TPU v7x, 256 devices: a whole 4x4x8 slice. The times are simulated.
256 devices in a mesh: dp: 4 (over x), seq: 8 (over z_lo, y), tensor: 8 (over z_hi, core).
Axes of the slice: x: 4, y: 4, z: 8 (z_hi: 4, z_lo: 2; z = z_hi * 2 + z_lo), core: 2. Of those that a mesh axis runs over, the one named last changes fastest.
Arguments:
- hidden: bfloat16 [4096, 28672], P(('dp', 'seq'), 'tensor'), may hold values from -6 to 6
- weight: bfloat16 [28672, 4096], P('tensor', 'seq'), may hold values from -0.03125 to 0.03125
- out_grad: bfloat16 [4096, 4096], P(('dp', 'tensor'), 'seq'), may hold values from -6 to 6
Outputs:
- output: bfloat16 [4096, 4096], P(('dp', 'tensor'), 'seq')
- grad_hidden: bfloat16 [4096, 28672], P(('dp', 'seq'), 'tensor')
- grad_weight: bfloat16 [28672, 4096], P('tensor', 'seq')
All inputs are finite; a program needn't handle non-finite values.
Results may differ from a plain program's by a relative error of at most 0.017.
Values may be sent and summed in bfloat16 or wider, within the bound.
A program may use at most 128 MiB of HBM per device.

v0:
```python
import jax
import jax.numpy as jnp
from jax import lax
from jax.sharding import PartitionSpec as P

HB = 512


def partner_2(shard, axis, distance):
    return lax.ppermute(shard, axis, [(i, i ^ 1 << distance) for i in range(lax.axis_size(axis))])


def walsh_table(table_order):
    matrix = jnp.ones((1, 1), jnp.float32)
    while matrix.shape[0] < table_order:
        matrix = jnp.concatenate(
            [jnp.concatenate([matrix, matrix], 1), jnp.concatenate([matrix, -matrix], 1)], 0
        )
    return matrix


def local_blocks(values, inner_table):
    row_count, feature_count = values.shape
    block_size = inner_table.shape[0]
    shaped = values.reshape(row_count, feature_count // block_size, block_size)
    if values.dtype == jnp.bfloat16:
        mixed_rows = jnp.einsum(
            "rbk,kl->rbl",
            shaped,
            inner_table.astype(jnp.bfloat16),
            preferred_element_type=jnp.float32,
        )
    else:
        mixed_rows = jnp.einsum("rbk,kl->rbl", shaped, inner_table, precision=lax.Precision.HIGHEST)
    return mixed_rows.reshape(row_count, feature_count)


def butterfly(values):
    axis_count = lax.axis_size("tensor")
    device_index = lax.axis_index("tensor")
    for bit_index in range(axis_count.bit_length() - 1):
        partner = partner_2(values.astype(jnp.bfloat16), "tensor", bit_index).astype(values.dtype)
        upper_half = device_index // (1 << bit_index) % 2 == 1
        values = jnp.where(upper_half, partner - values, values + partner)
    return values


def rotate(values, inner_table, norm_scale):
    return (butterfly(local_blocks(values, inner_table)) * norm_scale).astype(jnp.bfloat16)


def body(hidden, weight, out_grad):
    inner_table = walsh_table(HB)
    norm_scale = 1.0 / float(lax.axis_size("tensor") * HB) ** 0.5
    rotated = rotate(hidden, inner_table, norm_scale)
    gathered = lax.all_gather(rotated, "seq", axis=0, tiled=True)
    partial_sums = jnp.dot(gathered, weight, preferred_element_type=jnp.float32)
    output = lax.psum_scatter(
        partial_sums.astype(jnp.bfloat16), "tensor", scatter_dimension=0, tiled=True
    )
    grads_all = lax.all_gather(out_grad, "tensor", axis=0, tiled=True)
    token_total = hidden.shape[0] * lax.axis_size("seq") * lax.axis_size("dp")
    grad_term = lax.dot_general(
        gathered, grads_all, (((0,), (0,)), ((), ())), preferred_element_type=jnp.float32
    )
    grad_weight = lax.psum(
        (grad_term * (1.0 / float(token_total) ** 0.5)).astype(jnp.bfloat16), "dp"
    )
    rotated_grad = lax.psum_scatter(
        lax.dot_general(
            grads_all, weight, (((1,), (1,)), ((), ())), preferred_element_type=jnp.float32
        ).astype(jnp.bfloat16),
        "seq",
        scatter_dimension=0,
        tiled=True,
    ).astype(jnp.float32)
    grad_hidden = rotate(rotated_grad, inner_table, norm_scale)
    return (output, grad_hidden, grad_weight)


def solution(mesh):
    in_specs = (P(("dp", "seq"), "tensor"), P("tensor", "seq"), P(("dp", "tensor"), "seq"))
    out_specs = (P(("dp", "tensor"), "seq"), P(("dp", "seq"), "tensor"), P("tensor", "seq"))
    return jax.shard_map(body, mesh=mesh, in_specs=in_specs, out_specs=out_specs, check_vma=False)
```

profile of v0, /device:TPU:1, one launch (start us, length us, event | category | flops | bytes accessed | tf_op | source)
XLA Modules:
  0.0 447.1 jit_solution(14021014759159372248)
XLA Ops:
  7.2 0.7 all-gather.5.cloned.1.call-update
  7.9 36.3 %all-gather.5.cloned.1.call-done = bf16[1024,512]{1,0:T(8,128)(2,1)} async-done(((bf16[128,512]{1,0:T(8,128)(2,1)}), bf16[1024,512]{1,0:T(8,128)(2,1)}) %all-gather.5.cloned.1.call-update) | async-done | bytes 1048592 | tf_op jit(solution)/shard_map/all_gather | solution.py:61
  44.2 9.3 %convolution_convert_fusion = bf16[1024,3584]{1,0:T(8,128)(2,1)} fusion(bf16[1024,512]{1,0:T(8,128)(2,1)} %all-gather.5.cloned.1.call-done, bf16[3584,512]{1,0:T(8,128)(2,1)} %param.4), kind=kOutput, calls=%fused_computation | convolution fusion | flops 3761766400 | bytes 12058624 | tf_op jit(solution)/shard_map/dot_general | solution.py:70
  53.6 1.1 copy-done
  54.7 0.6 copy.11
  55.3 0.7 fusion.14
  56.0 1.0 bitcast_convert_fusion.1
  57.4 2.4 collective-permute-done
  59.7 1.2 fusion.13
  61.0 1.6 collective-permute-start.1
  62.5 41.3 %collective-permute-done.1 = bf16[128,3584]{0,1:T(8,128)(2,1)} collective-permute-done((bf16[128,3584]{0,1:T(8,128)(2,1)}, bf16[128,3584]{0,1:T(8,128)(2,1)}, u32[]{:S(2)}, u32[]{:S(2)}) %collective-permute-start.1) | collective-permute-done | bytes 917536 | tf_op jit(solution)/shard_map/ppermute | solution.py:10
  103.8 2.6 fusion.11
  106.5 2.7 collective-permute-start.2
  109.2 62.5 %collective-permute-done.2 = bf16[128,3584]{0,1:T(8,128)(2,1)} collective-permute-done((bf16[128,3584]{0,1:T(8,128)(2,1)}, bf16[128,3584]{0,1:T(8,128)(2,1)}, u32[]{:S(2)}, u32[]{:S(2)}) %collective-permute-start.2) | collective-permute-done | bytes 917536 | tf_op jit(solution)/shard_map/ppermute | solution.py:10
  171.7 3.2 fusion.4
  175.0 20.5 %reduce-scatter.5.cloned.1.call-done = bf16[128,3584]{1,0:T(8,128)(2,1)} async-done(((bf16[1024,3584]{1,0:T(8,128)(2,1)}), bf16[128,3584]{1,0:T(8,128)(2,1)}) %reduce-scatter.5.cloned.1.call-update) | async-done | bytes 917520 | tf_op jit(solution)/shard_map/reduce_scatter | solution.py:69
  195.5 1.5 copy.13
  197.0 3.1 fusion.15
  200.1 1.0 bitcast_convert_fusion
  201.5 79.5 %all-gather.3.cloned.1.call-done = bf16[1024,3584]{0,1:T(8,128)(2,1)} async-done(((bf16[128,3584]{0,1:T(8,128)(2,1)}), bf16[1024,3584]{0,1:T(8,128)(2,1)}) %all-gather.3.cloned.1.call-update) | async-done | bytes 7340048 | tf_op jit(solution)/shard_map/all_gather | solution.py:56
  281.0 9.1 %convolution_convert_fusion.1 = bf16[1024,512]{1,0:T(8,128)(2,1)} fusion(bf16[1024,3584]{0,1:T(8,128)(2,1)} %all-gather.3.cloned.1.call-done, bf16[3584,512]{1,0:T(8,128)(2,1)} %param.4), kind=kOutput, calls=%fused_computation.26 | convolution fusion | flops 3758620672 | bytes 12058624 | tf_op jit(solution)/shard_map/dot_general | solution.py:57
  290.2 1.2 fusion.12
  291.4 2.3 collective-permute-start.4
  293.7 8.5 %multiply_convert_fusion = bf16[3584,512]{1,0:T(8,128)(2,1)} fusion(bf16[1024,3584]{0,1:T(8,128)(2,1)} %all-gather.3.cloned.1.call-done, bf16[1024,512]{1,0:T(8,128)(2,1)S(1)} %copy-done.2), kind=kOutput, calls=%fused_computation.1 | convolution fusion | flops 3761766400 | bytes 12058624 | tf_op jit(solution)/shard_map/dot_general | solution.py:63
  302.2 41.2 %collective-permute-done.4 = bf16[128,3584]{0,1:T(8,128)(2,1)} collective-permute-done((bf16[128,3584]{0,1:T(8,128)(2,1)}, bf16[128,3584]{0,1:T(8,128)(2,1)}, u32[]{:S(2)}, u32[]{:S(2)}) %collective-permute-start.4) | collective-permute-done | bytes 917536 | tf_op jit(solution)/shard_map/ppermute | solution.py:10
  343.4 1.7 fusion.10
  345.1 6.5 %collective-permute-start.5 = (bf16[128,3584]{0,1:T(8,128)(2,1)S(1)}, bf16[128,3584]{0,1:T(8,128)(2,1)S(1)}, u32[]{:S(2)}, u32[]{:S(2)}) collective-permute-start(bf16[128,3584]{0,1:T(8,128)(2,1)S(1)} %fusion.10), channel_id=1, source_target_pairs={{0,4},{1,5},{2,6},{3,7},{4,0},{5,1},{6,2},{7,3},{8,12},{9,13},{10,... | collective-permute-start | bytes 2752520 | tf_op jit(solution)/shard_map/ppermute | solution.py:10
  351.6 40.0 %collective-permute-done.5 = bf16[128,3584]{0,1:T(8,128)(2,1)S(1)} collective-permute-done((bf16[128,3584]{0,1:T(8,128)(2,1)S(1)}, bf16[128,3584]{0,1:T(8,128)(2,1)S(1)}, u32[]{:S(2)}, u32[]{:S(2)}) %collective-permute-start.5) | collective-permute-done | bytes 917536 | tf_op jit(solution)/shard_map/ppermute | solution.py:10
  391.6 3.0 fusion.9
  394.6 2.2 copy.16
  396.8 39.6 %all-reduce.2.cloned.1.call-done = bf16[3584,512]{1,0:T(8,128)(2,1)} async-done(((bf16[3584,512]{1,0:T(8,128)(2,1)}), bf16[3584,512]{1,0:T(8,128)(2,1)}) %all-reduce.2.cloned.1.call-update) | async-done | bytes 3670032 | tf_op jit(solution)/shard_map/psum | solution.py:66
  436.4 4.1 copy.21
  (18 shorter events, 1.0 us)
Async XLA Ops:
  7.2 37.1 %all-gather.5.cloned.1.call-start = ((), (), s32[]{:S(2)}) async-start(), calls=%async_computation.4 | async-start | bytes 1179648 | tf_op jit(solution)/shard_map/all_gather | solution.py:61
  7.9 187.6 %reduce-scatter.5.cloned.1.call-start = ((), (), s32[]{:S(2)}) async-start(), calls=%async_computation.5 | async-start | bytes 8257536 | tf_op jit(solution)/shard_map/reduce_scatter | solution.py:69
  53.5 1.2 copy-start
  53.6 1.8 copy-start.1
  53.6 227.5 %all-gather.3.cloned.1.call-start = ((), (), s32[]{:S(2)}) async-start(), calls=%async_computation.2 | async-start | bytes 8257536 | tf_op jit(solution)/shard_map/all_gather | solution.py:56
  57.1 2.7 collective-permute-start
  61.0 42.9 %collective-permute-start.1 = (bf16[128,3584]{0,1:T(8,128)(2,1)}, bf16[128,3584]{0,1:T(8,128)(2,1)}, u32[]{:S(2)}, u32[]{:S(2)}) collective-permute-start(bf16[128,3584]{0,1:T(8,128)(2,1)} %fusion.13), channel_id=1, source_target_pairs={{0,2},{1,3},{2,0},{3,1},{4,6},{5,7},{6,4},{7,5},{8,10},{9,11},{10,... | collective-permute-start | bytes 2752520 | tf_op jit(solution)/shard_map/ppermute | solution.py:10
  106.5 65.2 %collective-permute-start.2 = (bf16[128,3584]{0,1:T(8,128)(2,1)}, bf16[128,3584]{0,1:T(8,128)(2,1)}, u32[]{:S(2)}, u32[]{:S(2)}) collective-permute-start(bf16[128,3584]{0,1:T(8,128)(2,1)} %fusion.11), channel_id=1, source_target_pairs={{0,4},{1,5},{2,6},{3,7},{4,0},{5,1},{6,2},{7,3},{8,12},{9,13},{10,... | collective-permute-start | bytes 2752520 | tf_op jit(solution)/shard_map/ppermute | solution.py:10
  175.0 221.8 %reduce-scatter.3.cloned.1.call-start = ((), (), s32[]{:S(2)}) async-start(), calls=%async_computation.3 | async-start | bytes 1179648 | tf_op jit(solution)/shard_map/reduce_scatter | solution.py:58
  201.1 89.1 %collective-permute-start.3 = (bf16[128,3584]{0,1:T(8,128)(2,1)}, bf16[128,3584]{0,1:T(8,128)(2,1)S(1)}, u32[]{:S(2)}, u32[]{:S(2)}) collective-permute-start(bf16[128,3584]{0,1:T(8,128)(2,1)} %bitcast_convert_fusion), channel_id=1, source_target_pairs={{0,1},{1,0},{2,3},{3,2},{4,5},{5,4},{6,7},{7,6},{8,9},{9,8},{10,11... | collective-permute-start | bytes 2752520 | tf_op jit(solution)/shard_map/ppermute | solution.py:10
  290.1 146.3 %all-reduce.2.cloned.1.call-start = ((), (), s32[]{:S(2)}) async-start(), calls=%async_computation.6 | async-start | bytes 7340032 | tf_op jit(solution)/shard_map/psum | solution.py:66
  290.2 3.5 copy-start.2
  291.4 52.0 %collective-permute-start.4 = (bf16[128,3584]{0,1:T(8,128)(2,1)}, bf16[128,3584]{0,1:T(8,128)(2,1)}, u32[]{:S(2)}, u32[]{:S(2)}) collective-permute-start(bf16[128,3584]{0,1:T(8,128)(2,1)} %fusion.12), channel_id=1, source_target_pairs={{0,2},{1,3},{2,0},{3,1},{4,6},{5,7},{6,4},{7,5},{8,10},{9,11},{10,... | collective-permute-start | bytes 2752520 | tf_op jit(solution)/shard_map/ppermute | solution.py:10
  345.1 46.4 %collective-permute-start.5 = (bf16[128,3584]{0,1:T(8,128)(2,1)S(1)}, bf16[128,3584]{0,1:T(8,128)(2,1)S(1)}, u32[]{:S(2)}, u32[]{:S(2)}) collective-permute-start(bf16[128,3584]{0,1:T(8,128)(2,1)S(1)} %fusion.10), channel_id=1, source_target_pairs={{0,4},{1,5},{2,6},{3,7},{4,0},{5,1},{6,2},{7,3},{8,12},{9,13},{10,... | collective-permute-start | bytes 2752520 | tf_op jit(solution)/shard_map/ppermute | solution.py:10
Sparse Core Ops, SparseCore 0:
  9.8 34.3 all-gather.4
  53.7 141.7 reduce-scatter.4
  197.8 83.2 all-gather.2
  290.3 50.2 reduce-scatter.2
  343.4 93.0 all-reduce.1
where the time goes:
time: 447 us
  waiting for transfers between devices  364 us (81%)
  matrix products  30.6 us (7%)
  other arithmetic  15 us (3%)
  starting transfers between devices  13.9 us (3%)
  between operations  13.8 us (3%)
  local copies, waits for them, and re-layouts  9.58 us (2%)
    ppermute x6, waiting for transfers between devices, partner_2(): lax.ppermute(shard, axis, [(i, i ^ 1 << distance) for i in range(lax.axis...  187 us
    all_gather x1, waiting for transfers between devices, body(): gathered = lax.all_gather(rotated, 'seq', axis=0, tiled=True)  79.5 us
    psum x1, waiting for transfers between devices, body(): lax.psum((grad_term * (1.0 / float(token_total) ** 0.5)).astype(jnp.bfloa...  39.6 us
    all_gather x1, waiting for transfers between devices, body(): grads_all = lax.all_gather(out_grad, 'tensor', axis=0, tiled=True)  36.3 us
    reduce_scatter x1, waiting for transfers between devices, body(): lax.psum_scatter(lax.dot_general(grads_all, weight, (((1,), (1,)), ((), (...  20.5 us
    ppermute x6, starting transfers between devices, partner_2(): lax.ppermute(shard, axis, [(i, i ^ 1 << distance) for i in range(lax.axis...  13.7 us
    dot_general x1, matrix products, body(): lax.dot_general(grads_all, weight, (((1,), (1,)), ((), ())), preferred_el...  9.3 us
    dot_general x1, matrix products, body(): partial_sums = jnp.dot(gathered, weight, preferred_element_type=jnp.float32)  9.08 us
  transfers between devices with their start and end apart: 11, of which 9 were waited for; matrix products, arithmetic and copies ran while one was open for 9% of the time, Pallas kernels for 0%

commit v1 on v0

--- a/solution.py
+++ b/solution.py
@@ -58,7 +58,9 @@
     output = lax.psum_scatter(
         partial_sums.astype(jnp.bfloat16), "tensor", scatter_dimension=0, tiled=True
     )
-    grads_all = lax.all_gather(out_grad, "tensor", axis=0, tiled=True)
+    grads_all = jnp.concatenate(
+        lax.all_to_all(jnp.stack([out_grad] * lax.axis_size("tensor")), "tensor", 0, 0), axis=0
+    )
     token_total = hidden.shape[0] * lax.axis_size("seq") * lax.axis_size("dp")
     grad_term = lax.dot_general(
         gathered, grads_all, (((0,), (0,)), ((), ())), preferred_element_type=jnp.float32

time: 447 us -> 450 us (level)
  waiting for transfers between devices: 364 us -> 329 us
  blocking collectives: 0 us -> 34.7 us
    all_gather x1 -> x0, waiting for transfers between devices: 36.3 us -> none  [body(): grads_all = lax.all_gather(out_grad, 'tensor', axis=0, tiled=True)]
    all_to_all x0 -> x1, blocking collectives: none -> 34.7 us  [body(): lax.all_to_all(jnp.stack([out_grad] * lax.axis_size('tensor')), 'tensor',...]
    unnamed x9 -> x11, local copies, waits for them, and re-layouts: 8.03 us -> 9 us
  transfers between devices with their start and end apart: 11 -> 10, of which waited for: 9 -> 8; matrix products, arithmetic and copies ran while one was open for 9% -> 9% of each run, Pallas kernels for 0% -> 0%
where the time goes in v1:
time: 450 us; the launch traced here: 449 us
  waiting for transfers between devices  329 us (73%)
  blocking collectives  34.7 us (8%)
  matrix products  29.7 us (7%)
  starting transfers between devices  15.7 us (3%)
  other arithmetic  15.1 us (3%)
  between operations  13.8 us (3%)
  local copies, waits for them, and re-layouts  11.5 us (3%)
    ppermute x6, waiting for transfers between devices, partner_2(): lax.ppermute(shard, axis, [(i, i ^ 1 << distance) for i in range(lax.axis...  189 us
    all_gather x1, waiting for transfers between devices, body(): gathered = lax.all_gather(rotated, 'seq', axis=0, tiled=True)  79.5 us
    psum x1, waiting for transfers between devices, body(): lax.psum((grad_term * (1.0 / float(token_total) ** 0.5)).astype(jnp.bfloa...  39.7 us
    all_to_all x1, blocking collectives, body(): lax.all_to_all(jnp.stack([out_grad] * lax.axis_size('tensor')), 'tensor',...  34.7 us
    reduce_scatter x1, waiting for transfers between devices, body(): lax.psum_scatter(lax.dot_general(grads_all, weight, (((1,), (1,)), ((), (...  20.3 us
    ppermute x6, starting transfers between devices, partner_2(): lax.ppermute(shard, axis, [(i, i ^ 1 << distance) for i in range(lax.axis...  15.5 us
    dot_general x1, matrix products, body(): partial_sums = jnp.dot(gathered, weight, preferred_element_type=jnp.float32)  9.11 us
    unnamed x11, local copies, waits for them, and re-layouts  9 us
  transfers between devices with their start and end apart: 10, of which 8 were waited for; matrix products, arithmetic and copies ran while one was open for 9% of the time, Pallas kernels for 0%

profile of v1, /device:TPU:1, one launch (start us, length us, event | category | flops | bytes accessed | tf_op | source)
XLA Modules:
  0.0 449.2 jit_solution(4942421829117687060)
XLA Ops:
  7.2 1.0 stack.2
  8.2 34.7 %all_to_all.5 = bf16[8,128,512]{2,1,0:T(8,128)(2,1)S(1)} all-to-all(bf16[8,128,512]{2,1,0:T(8,128)(2,1)S(1)} %stack.2), channel_id=1, replica_groups=mesh['dp'=4,'seq'=8,'tensor'=8] {'tensor'}, dimensions={0} | all-to-all | bytes 2097152 | tf_op jit(solution)/shard_map/all_to_all | solution.py:62
  42.9 1.0 copy-done
  43.9 8.3 %convolution_convert_fusion = bf16[1024,3584]{1,0:T(8,128)(2,1)} fusion(bf16[1024,512]{1,0:T(8,128)(2,1)S(1)} %bitcast.37, bf16[3584,512]{1,0:T(8,128)(2,1)} %param.4), kind=kOutput, calls=%fused_computation | convolution fusion | flops 3761766400 | bytes 12058624 | tf_op jit(solution)/shard_map/dot_general | solution.py:72
  52.3 1.1 copy-done.2
  54.7 1.0 bitcast_convert_fusion.1
  55.7 4.3 collective-permute-start
  60.0 2.3 collective-permute-done
  62.3 1.2 fusion.13
  64.1 41.6 %collective-permute-done.1 = bf16[128,3584]{0,1:T(8,128)(2,1)} collective-permute-done((bf16[128,3584]{0,1:T(8,128)(2,1)}, bf16[128,3584]{0,1:T(8,128)(2,1)}, u32[]{:S(2)}, u32[]{:S(2)}) %collective-permute-start.1) | collective-permute-done | bytes 917536 | tf_op jit(solution)/shard_map/ppermute | solution.py:10
  105.7 2.6 fusion.11
  108.4 1.3 collective-permute-start.2
  109.6 63.9 %collective-permute-done.2 = bf16[128,3584]{0,1:T(8,128)(2,1)} collective-permute-done((bf16[128,3584]{0,1:T(8,128)(2,1)}, bf16[128,3584]{0,1:T(8,128)(2,1)}, u32[]{:S(2)}, u32[]{:S(2)}) %collective-permute-start.2) | collective-permute-done | bytes 917536 | tf_op jit(solution)/shard_map/ppermute | solution.py:10
  173.5 3.2 fusion.4
  176.8 20.3 %reduce-scatter.5.cloned.1.call-done = bf16[128,3584]{1,0:T(8,128)(2,1)} async-done(((bf16[1024,3584]{1,0:T(8,128)(2,1)}), bf16[128,3584]{1,0:T(8,128)(2,1)}) %reduce-scatter.5.cloned.1.call-update) | async-done | bytes 917520 | tf_op jit(solution)/shard_map/reduce_scatter | solution.py:71
  197.1 1.5 copy.13
  198.7 3.1 fusion.15
  201.7 1.1 bitcast_convert_fusion
  202.8 0.7 collective-permute-start.3
  203.6 79.5 %all-gather.2.cloned.1.call-done = bf16[1024,3584]{0,1:T(8,128)(2,1)} async-done(((bf16[128,3584]{0,1:T(8,128)(2,1)}), bf16[1024,3584]{0,1:T(8,128)(2,1)}) %all-gather.2.cloned.1.call-update) | async-done | bytes 7340048 | tf_op jit(solution)/shard_map/all_gather | solution.py:56
  283.1 9.1 %convolution_convert_fusion.1 = bf16[1024,512]{1,0:T(8,128)(2,1)} fusion(bf16[1024,3584]{0,1:T(8,128)(2,1)} %all-gather.2.cloned.1.call-done, bf16[3584,512]{1,0:T(8,128)(2,1)} %param.4), kind=kOutput, calls=%fused_computation.26 | convolution fusion | flops 3758620672 | bytes 12058624 | tf_op jit(solution)/shard_map/dot_general | solution.py:57
  292.3 1.2 fusion.12
  293.5 2.3 collective-permute-start.4
  295.8 8.5 %multiply_convert_fusion = bf16[3584,512]{1,0:T(8,128)(2,1)} fusion(bf16[1024,3584]{0,1:T(8,128)(2,1)} %all-gather.2.cloned.1.call-done, bf16[1024,512]{1,0:T(8,128)(2,1)S(1)} %bitcast.38), kind=kOutput, calls=%fused_computation.1 | convolution fusion | flops 3761766400 | bytes 12058624 | tf_op jit(solution)/shard_map/dot_general | solution.py:65
  304.3 41.2 %collective-permute-done.4 = bf16[128,3584]{0,1:T(8,128)(2,1)} collective-permute-done((bf16[128,3584]{0,1:T(8,128)(2,1)}, bf16[128,3584]{0,1:T(8,128)(2,1)}, u32[]{:S(2)}, u32[]{:S(2)}) %collective-permute-start.4) | collective-permute-done | bytes 917536 | tf_op jit(solution)/shard_map/ppermute | solution.py:10
  345.5 1.7 fusion.10
  347.2 6.4 %collective-permute-start.5 = (bf16[128,3584]{0,1:T(8,128)(2,1)S(1)}, bf16[128,3584]{0,1:T(8,128)(2,1)S(1)}, u32[]{:S(2)}, u32[]{:S(2)}) collective-permute-start(bf16[128,3584]{0,1:T(8,128)(2,1)S(1)} %fusion.10), channel_id=1, source_target_pairs={{0,4},{1,5},{2,6},{3,7},{4,0},{5,1},{6,2},{7,3},{8,12},{9,13},{10,... | collective-permute-start | bytes 2752520 | tf_op jit(solution)/shard_map/ppermute | solution.py:10
  353.7 40.0 %collective-permute-done.5 = bf16[128,3584]{0,1:T(8,128)(2,1)S(1)} collective-permute-done((bf16[128,3584]{0,1:T(8,128)(2,1)S(1)}, bf16[128,3584]{0,1:T(8,128)(2,1)S(1)}, u32[]{:S(2)}, u32[]{:S(2)}) %collective-permute-start.5) | collective-permute-done | bytes 917536 | tf_op jit(solution)/shard_map/ppermute | solution.py:10
  393.6 3.0 fusion.9
  396.6 2.2 copy.16
  398.8 39.7 %all-reduce.2.cloned.1.call-done = bf16[3584,512]{1,0:T(8,128)(2,1)} async-done(((bf16[3584,512]{1,0:T(8,128)(2,1)}), bf16[3584,512]{1,0:T(8,128)(2,1)}) %all-reduce.2.cloned.1.call-update) | async-done | bytes 3670032 | tf_op jit(solution)/shard_map/psum | solution.py:68
  438.5 4.1 copy.21
  (19 shorter events, 2.1 us)
Async XLA Ops:
  7.2 190.0 %reduce-scatter.5.cloned.1.call-start = ((), (), s32[]{:S(2)}) async-start(), calls=%async_computation.5 | async-start | bytes 8257536 | tf_op jit(solution)/shard_map/reduce_scatter | solution.py:71
  42.9 1.0 copy-start
  52.2 1.2 copy-start.2
  52.2 1.8 copy-start.3
  52.3 230.8 %all-gather.2.cloned.1.call-start = ((), (), s32[]{:S(2)}) async-start(), calls=%async_computation.3 | async-start | bytes 8257536 | tf_op jit(solution)/shard_map/all_gather | solution.py:56
  55.7 6.6 %collective-permute-start = (bf16[128,3584]{0,1:T(8,128)(2,1)}, bf16[128,3584]{0,1:T(8,128)(2,1)S(1)}, u32[]{:S(2)}, u32[]{:S(2)}) collective-permute-start(bf16[128,3584]{0,1:T(8,128)(2,1)} %bitcast_convert_fusion.1), channel_id=1, source_target_pairs={{0,1},{1,0},{2,3},{3,2},{4,5},{5,4},{6,7},{7,6},{8,9},{9,8},{10,11... | collective-permute-start | bytes 2752520 | tf_op jit(solution)/shard_map/ppermute | solution.py:10
  63.6 42.1 %collective-permute-start.1 = (bf16[128,3584]{0,1:T(8,128)(2,1)}, bf16[128,3584]{0,1:T(8,128)(2,1)}, u32[]{:S(2)}, u32[]{:S(2)}) collective-permute-start(bf16[128,3584]{0,1:T(8,128)(2,1)} %fusion.13), channel_id=1, source_target_pairs={{0,2},{1,3},{2,0},{3,1},{4,6},{5,7},{6,4},{7,5},{8,10},{9,11},{10,... | collective-permute-start | bytes 2752520 | tf_op jit(solution)/shard_map/ppermute | solution.py:10
  108.4 65.1 %collective-permute-start.2 = (bf16[128,3584]{0,1:T(8,128)(2,1)}, bf16[128,3584]{0,1:T(8,128)(2,1)}, u32[]{:S(2)}, u32[]{:S(2)}) collective-permute-start(bf16[128,3584]{0,1:T(8,128)(2,1)} %fusion.11), channel_id=1, source_target_pairs={{0,4},{1,5},{2,6},{3,7},{4,0},{5,1},{6,2},{7,3},{8,12},{9,13},{10,... | collective-permute-start | bytes 2752520 | tf_op jit(solution)/shard_map/ppermute | solution.py:10
  176.7 222.1 %reduce-scatter.3.cloned.1.call-start = ((), (), s32[]{:S(2)}) async-start(), calls=%async_computation.4 | async-start | bytes 1179648 | tf_op jit(solution)/shard_map/reduce_scatter | solution.py:58
  202.8 89.4 %collective-permute-start.3 = (bf16[128,3584]{0,1:T(8,128)(2,1)}, bf16[128,3584]{0,1:T(8,128)(2,1)S(1)}, u32[]{:S(2)}, u32[]{:S(2)}) collective-permute-start(bf16[128,3584]{0,1:T(8,128)(2,1)} %bitcast_convert_fusion), channel_id=1, source_target_pairs={{0,1},{1,0},{2,3},{3,2},{4,5},{5,4},{6,7},{7,6},{8,9},{9,8},{10,11... | collective-permute-start | bytes 2752520 | tf_op jit(solution)/shard_map/ppermute | solution.py:10
  292.2 146.3 %all-reduce.2.cloned.1.call-start = ((), (), s32[]{:S(2)}) async-start(), calls=%async_computation.6 | async-start | bytes 7340032 | tf_op jit(solution)/shard_map/psum | solution.py:68
  292.3 3.5 copy-start.1
  293.5 52.0 %collective-permute-start.4 = (bf16[128,3584]{0,1:T(8,128)(2,1)}, bf16[128,3584]{0,1:T(8,128)(2,1)}, u32[]{:S(2)}, u32[]{:S(2)}) collective-permute-start(bf16[128,3584]{0,1:T(8,128)(2,1)} %fusion.12), channel_id=1, source_target_pairs={{0,2},{1,3},{2,0},{3,1},{4,6},{5,7},{6,4},{7,5},{8,10},{9,11},{10,... | collective-permute-start | bytes 2752520 | tf_op jit(solution)/shard_map/ppermute | solution.py:10
  347.2 46.4 %collective-permute-start.5 = (bf16[128,3584]{0,1:T(8,128)(2,1)S(1)}, bf16[128,3584]{0,1:T(8,128)(2,1)S(1)}, u32[]{:S(2)}, u32[]{:S(2)}) collective-permute-start(bf16[128,3584]{0,1:T(8,128)(2,1)S(1)} %fusion.10), channel_id=1, source_target_pairs={{0,4},{1,5},{2,6},{3,7},{4,0},{5,1},{6,2},{7,3},{8,12},{9,13},{10,... | collective-permute-start | bytes 2752520 | tf_op jit(solution)/shard_map/ppermute | solution.py:10
Sparse Core Ops, SparseCore 0:
  52.4 144.7 reduce-scatter.4
  199.4 83.6 all-gather.1
  292.3 50.2 reduce-scatter.2
  345.4 93.0 all-reduce.1
